TPU v7x, 32 devices: a whole 2x2x4 slice. The times are simulated.
32 devices in a mesh: head: 4 (over x, core), tok: 8 (over z, y).
Axes of the slice: x: 2, y: 2, z: 4, core: 2. Of those that a mesh axis runs over, the one named last changes fastest.
Arguments:
- tokens: bfloat16 [512, 4096], P('tok'), may hold values from -6 to 6
- attn_gain: float32 [4096], replicated, may hold values from 0.5 to 1.5
- q_weight: bfloat16 [4096, 2048], P('tok', 'head'), may hold values from -0.09375 to 0.09375
- k_weight: bfloat16 [4096, 512], P('tok', 'head'), may hold values from -0.09375 to 0.09375
- v_weight: bfloat16 [4096, 512], P('tok', 'head'), may hold values from -0.09375 to 0.09375
- output_matrix: bfloat16 [2048, 4096], P('head', 'tok'), may hold values from -0.125 to 0.125
- key_cache: bfloat16 [64, 256, 512], P('tok', None, 'head'), may hold values from -400 to 400
- value_cache: bfloat16 [64, 256, 512], P('tok', None, 'head'), may hold values from -6 to 6
- cache_lengths: int32 [64], P('tok'), may hold values from 1 to 256
- row_request_index: int32 [8, 64], P('tok'), may hold values from 0 to 7, never falling along the last dimension, each value on 1 to 32 neighbouring positions
- ffn_gain: float32 [4096], replicated, may hold values from 0.5 to 1.5
- router_weight: bfloat16 [4096, 8], replicated, may hold values from -0.09375 to 0.09375
- routes: int32 [512, 2], P('tok'), may hold values from 0 to 7, all different within a row; in each aligned block of 64 rows (0 to 63, 64 to 127, ...) at most 18 rows name the same one
- gate_weight: bfloat16 [8, 4096, 14336], P('tok', None, 'head'), may hold values from -0.09375 to 0.09375
- up_weight: bfloat16 [8, 4096, 14336], P('tok', None, 'head'), may hold values from -0.09375 to 0.09375
- down_weight: bfloat16 [8, 14336, 4096], P('tok', None, 'head'), may hold values from -0.046875 to 0.046875
Outputs:
- layer_out: bfloat16 [512, 4096], P('tok', 'head')
Inputs may be any that keep to these rules, and one draw needn't show every extreme that they name: `row_request_index`: within the rows of one index of tok the request number never falls, every request has 1 to 32 rows, and one has exactly 32. `routes`: the two experts of a row differ; in the rows of one index of tok no expert is named more than 18 times, and that bound is reached.
All inputs are finite; a program needn't handle non-finite values.
Results may differ from a plain program's by a relative error of at most 0.012.
The roundings to bfloat16 on the way count: a program that leaves them out, or rounds other values in their place, can miss the bound.
Values may be sent and summed in bfloat16 or wider, within the bound.
A program may use at most 256 MiB of HBM per device.

v0:
```python
import jax
import jax.numpy as jnp
from jax import lax
from jax.sharding import PartitionSpec as P

D = 4096
HD = 128
Q_HEADS = 16
KV_HEADS = 4
EXPERTS = 8
CAP = 18
epsilon = 1e-05
rope_base = 1000000.0


def rms_norm(values, gain):
    values = values.astype(jnp.float32)
    factor = lax.rsqrt(jnp.mean(values * values, axis=-1, keepdims=True) + epsilon)
    return (values * factor * gain).astype(jnp.bfloat16)


def rotate(values, positions):
    half = values.shape[-1] // 2
    freqs = rope_base ** (-jnp.arange(half, dtype=jnp.float32) * 2.0 / values.shape[-1])
    angles = positions.astype(jnp.float32)[:, None] * freqs[None, :]
    cosine = jnp.concatenate([jnp.cos(angles), jnp.cos(angles)], axis=-1)[:, None, :]
    sine = jnp.concatenate([jnp.sin(angles), jnp.sin(angles)], axis=-1)[:, None, :]
    turned = jnp.concatenate([-values[..., half:], values[..., :half]], axis=-1)
    return values * cosine + turned * sine


def own_lengths(segment, lengths):
    match = segment[:, None] == jnp.arange(lengths.shape[0], dtype=jnp.int32)[None, :]
    return jnp.sum(jnp.where(match, lengths[None, :], 0), axis=1)


def row_positions(segment, lengths):
    count = segment.shape[0]
    order = jnp.arange(count, dtype=jnp.int32)
    before = jnp.sum((segment[None, :] < segment[:, None]).astype(jnp.int32), axis=1)
    return own_lengths(segment, lengths) + order - before


def attend(queries, new_keys, new_values, key_cache, value_cache, segment, lengths):
    count, kv_local, group, size = queries.shape
    requests, slots, _ = key_cache.shape
    keys = jnp.concatenate([key_cache.reshape(requests * slots, kv_local, size), new_keys], axis=0)
    values = jnp.concatenate(
        [value_cache.reshape(requests * slots, kv_local, size), new_values], axis=0
    )
    slot_index = jnp.arange(requests * slots, dtype=jnp.int32)
    slot_request = slot_index // slots
    slot_place = slot_index % slots
    limit = own_lengths(segment, lengths)
    cache_valid = (slot_request[None, :] == segment[:, None]) & (
        slot_place[None, :] < limit[:, None]
    )
    order = jnp.arange(count, dtype=jnp.int32)
    new_valid = (segment[None, :] == segment[:, None]) & (order[None, :] <= order[:, None])
    allowed = jnp.concatenate([cache_valid, new_valid], axis=1)
    scores = jnp.einsum("rhgd,khd->hgrk", queries, keys, preferred_element_type=jnp.float32)
    scores = scores / jnp.sqrt(jnp.float32(size))
    scores = jnp.where(allowed[None, None], scores, jnp.float32(-1e30))
    highest = jnp.max(scores, axis=-1, keepdims=True)
    weights = jnp.exp(scores - highest)
    probs = (weights / jnp.sum(weights, axis=-1, keepdims=True)).astype(jnp.bfloat16)
    result = jnp.einsum("hgrk,khd->rhgd", probs, values, preferred_element_type=jnp.float32)
    return result.astype(jnp.bfloat16).reshape(count, kv_local * group * size)


def slot_table(chosen):
    flat = chosen.reshape(-1)
    onehot = (flat[:, None] == jnp.arange(EXPERTS, dtype=jnp.int32)[None, :]).astype(jnp.int32)
    earlier = jnp.cumsum(onehot, axis=0) - onehot
    place = jnp.sum(earlier * onehot, axis=1)
    return flat * CAP + place


def fill_slots(normed_rows, places):
    copies = normed_rows[jnp.arange(places.shape[0], dtype=jnp.int32) // 2]
    return jnp.zeros((EXPERTS * CAP, normed_rows.shape[1]), jnp.bfloat16).at[places].set(copies)


def gate_shares(normed_rows, router_weight, chosen):
    logits = jnp.dot(normed_rows, router_weight, preferred_element_type=jnp.float32)
    match = chosen[:, :, None] == jnp.arange(EXPERTS, dtype=jnp.int32)[None, None, :]
    picked = jnp.sum(jnp.where(match, logits[:, None, :], jnp.float32(0.0)), axis=-1)
    return jax.nn.sigmoid(picked - picked[:, ::-1])


def shards(
    tokens,
    attn_gain,
    q_weight,
    k_weight,
    v_weight,
    output_matrix,
    key_cache,
    value_cache,
    cache_lengths,
    row_request_index,
    ffn_gain,
    router_weight,
    routes,
    gate_weight,
    up_weight,
    down_weight,
):
    count = tokens.shape[0]
    group = Q_HEADS // KV_HEADS
    normed = rms_norm(tokens, attn_gain)
    q_full, k_full, v_full, o_full = (
        lax.all_gather(q_weight, "tok", axis=0, tiled=True),
        lax.all_gather(k_weight, "tok", axis=0, tiled=True),
        lax.all_gather(v_weight, "tok", axis=0, tiled=True),
        lax.all_gather(output_matrix, "tok", axis=1, tiled=True),
    )
    kv_local = k_full.shape[1] // HD
    queries = jnp.dot(normed, q_full, preferred_element_type=jnp.float32)
    keys_new = jnp.dot(normed, k_full, preferred_element_type=jnp.float32)
    values_new = jnp.dot(normed, v_full, preferred_element_type=jnp.float32)
    segment = row_request_index[0]
    positions = row_positions(segment, cache_lengths)
    queries = rotate(queries.reshape(count, kv_local * group, HD), positions).astype(jnp.bfloat16)
    queries = queries.reshape(count, kv_local, group, HD)
    keys_new = rotate(keys_new.reshape(count, kv_local, HD), positions).astype(jnp.bfloat16)
    values_new = values_new.astype(jnp.bfloat16).reshape(count, kv_local, HD)
    attn = attend(queries, keys_new, values_new, key_cache, value_cache, segment, cache_lengths)
    partial_mix = jnp.dot(attn, o_full, preferred_element_type=jnp.float32)
    mixed = lax.psum(partial_mix, "head")
    hidden_activation = tokens.astype(jnp.float32) + mixed
    normed_ffn = rms_norm(hidden_activation, ffn_gain)
    shares = gate_shares(normed_ffn, router_weight, routes)
    places = slot_table(routes)
    buffer = fill_slots(normed_ffn, places)
    owners = lax.axis_size("tok")
    slices = owners // EXPERTS
    quarter = down_weight.shape[2]
    head_index = lax.axis_index("head")
    outgoing = jnp.broadcast_to(
        buffer.reshape(EXPERTS, 1, CAP, D), (EXPERTS, slices, CAP, D)
    ).reshape(owners, CAP, D)
    arrived = lax.all_to_all(outgoing, "tok", split_axis=0, concat_axis=0, tiled=True)
    active = jnp.einsum("tcd,df->tcf", arrived, gate_weight[0], preferred_element_type=jnp.float32)
    linear = jnp.einsum("tcd,df->tcf", arrived, up_weight[0], preferred_element_type=jnp.float32)
    hidden = (jax.nn.silu(active) * linear).astype(jnp.bfloat16)
    hidden_all = lax.all_gather(hidden, "head", axis=2, tiled=True)
    output = jnp.einsum(
        "tcf,fd->tcd", hidden_all, down_weight[0], preferred_element_type=jnp.float32
    )
    layer_results = output.astype(jnp.bfloat16)
    returned = lax.all_to_all(layer_results, "tok", split_axis=0, concat_axis=0, tiled=True)
    summed = jnp.sum(returned.reshape(EXPERTS, slices, CAP, quarter).astype(jnp.float32), axis=1)
    summed = summed.reshape(EXPERTS * CAP, quarter)
    picked = jnp.take(summed, places, axis=0).reshape(count, 2, quarter)
    mixture = jnp.sum(shares[:, :, None] * picked, axis=1)
    residual = lax.dynamic_slice_in_dim(hidden_activation, head_index * quarter, quarter, 1)
    return (residual + mixture).astype(jnp.bfloat16)


def solution(mesh):
    in_specs = (
        P("tok", None),
        P(),
        P("tok", "head"),
        P("tok", "head"),
        P("tok", "head"),
        P("head", "tok"),
        P("tok", None, "head"),
        P("tok", None, "head"),
        P("tok"),
        P("tok", None),
        P(),
        P(),
        P("tok", None),
        P("tok", None, "head"),
        P("tok", None, "head"),
        P("tok", None, "head"),
    )
    out_specs = P("tok", "head")
    return jax.shard_map(shards, mesh=mesh, in_specs=in_specs, out_specs=out_specs, check_vma=False)
```

profile of v0, /device:TPU:0, one launch (start us, length us, event | category | flops | bytes accessed | tf_op | source)
XLA Modules:
  0.0 441.3 jit_solution(15756063312826419682)
XLA Ops:
  11.5 0.9 convert_reduce_fusion
  13.2 1.2 fusion.21
  14.4 0.8 fusion.42
  15.7 36.7 %all-gather.6.cloned.1.call-done = bf16[4096,128]{1,0:T(8,128)(2,1)} async-done(((bf16[512,128]{1,0:T(8,128)(2,1)}), bf16[4096,128]{1,0:T(8,128)(2,1)}) %all-gather.6.cloned.1.call-update) | async-done | bytes 1048592 | tf_op jit(solution)/shard_map/all_gather | solution.py:115
  52.4 1.6 fusion.20
  54.0 39.5 %all-gather.8.cloned.1.call-done = bf16[4096,128]{1,0:T(8,128)(2,1)} async-done(((bf16[512,128]{1,0:T(8,128)(2,1)}), bf16[4096,128]{1,0:T(8,128)(2,1)}) %all-gather.8.cloned.1.call-update) | async-done | bytes 1048592 | tf_op jit(solution)/shard_map/all_gather | solution.py:114
  93.4 1.6 fusion.57
  95.2 72.5 %all-gather.10.cloned.1.call-done = bf16[4096,512]{1,0:T(8,128)(2,1)} async-done(((bf16[512,512]{1,0:T(8,128)(2,1)}), bf16[4096,512]{1,0:T(8,128)(2,1)}) %all-gather.10.cloned.1.call-update) | async-done | bytes 4194320 | tf_op jit(solution)/shard_map/all_gather | solution.py:113
  167.8 3.1 fusion.55
  172.9 70.0 %all-gather.12.cloned.1.call-done = bf16[512,4096]{1,0:T(8,128)(2,1)} async-done(((bf16[512,512]{1,0:T(8,128)(2,1)}), bf16[512,4096]{1,0:T(8,128)(2,1)}) %all-gather.12.cloned.1.call-update) | async-done | bytes 4194320 | tf_op jit(solution)/shard_map/all_gather | solution.py:116
  243.0 4.0 fusion.33
  247.3 34.1 %all-reduce.2.cloned.1.call-done = f32[64,4096]{1,0:T(8,128)} async-done(((f32[64,4096]{1,0:T(8,128)}), f32[64,4096]{1,0:T(8,128)}) %all-reduce.2.cloned.1.call-update) | async-done | bytes 1048592 | tf_op jit(solution)/shard_map/psum | solution.py:130
  281.4 1.5 multiply_reduce_fusion
  283.1 6.2 %scatter_custom_fusion = bf16[144,4096]{1,0:T(8,128)(2,1)} fusion(s32[128]{0:T(128)S(1)} %fusion.52, bf16[64,4096]{1,0:T(8,128)(2,1)S(1)} %multiply_convert_fusion, s32[1024]{0:T(1024)S(1)} %pad_clamp_fusion.1, bf16[]{:T(256)} %constant.104.clone.1), kind=kCustom, calls=%fused_computation.29 | custom fusion | bytes 1179650 | tf_op jit(solution)/shard_map/scatter | solution.py:81
  289.2 1.4 reshape_reshape.3
  290.7 41.9 %all_to_all.10 = bf16[8,18,4096]{2,1,0:T(8,128)(2,1)S(1)} all-to-all(bf16[8,18,4096]{2,1,0:T(8,128)(2,1)S(1)} %reshape_reshape.3), channel_id=1, replica_groups=mesh['head'=4,'tok'=8] {'tok'}, dimensions={0} | all-to-all | bytes 2359296 | tf_op jit(solution)/shard_map/all_to_all | solution.py:143
  332.6 12.5 %fusion.4 = f32[8,18,3584]{2,1,0:T(8,128)S(1)} fusion(bf16[8,18,4096]{2,1,0:T(8,128)(2,1)S(1)} %all_to_all.10, bf16[1,4096,3584]{2,1,0:T(8,128)(2,1)} %param.29), kind=kOutput, calls=%fused_computation.7 | convolution fusion | flops 4227858432 | bytes 32604160 | tf_op jit(solution)/shard_map/tcd,df->tcf/dot_general | solution.py:144
  345.1 13.5 %fusion.9 = bf16[8,18,3584]{2,1,0:T(8,128)(2,1)} fusion(bf16[8,18,4096]{2,1,0:T(8,128)(2,1)S(1)} %all_to_all.10, bf16[1,4096,3584]{2,1,0:T(8,128)(2,1)} %param.30, f32[8,18,3584]{2,1,0:T(8,128)S(1)} %fusion.4), kind=kOutput, calls=%fused_computation.10 | convolution fusion | flops 4230955008 | bytes 33636352 | tf_op jit(solution)/shard_map/tcd,df->tcf/dot_general | solution.py:145
  359.0 40.4 %all-gather.14.cloned.1.call-done = bf16[8,18,14336]{2,1,0:T(8,128)(2,1)} async-done(((bf16[8,18,3584]{2,1,0:T(8,128)(2,1)}), bf16[8,18,14336]{2,1,0:T(8,128)(2,1)}) %all-gather.14.cloned.1.call-update) | async-done | bytes 4128784 | tf_op jit(solution)/shard_map/all_gather | solution.py:147
  399.4 14.7 %fusion.15 = bf16[8,18,1024]{2,1,0:T(8,128)(2,1)} fusion(bf16[8,18,14336]{2,1,0:T(8,128)(2,1)} %all-gather.14.cloned.1.call-done, bf16[1,14336,1024]{2,1,0:T(8,128)(2,1)} %param.31), kind=kOutput, calls=%fused_computation.20 | convolution fusion | flops 4228005888 | bytes 33783808 | tf_op jit(solution)/shard_map/tcf,fd->tcd/dot_general | solution.py:148
  414.1 5.5 %all-to-all-start.1 = ((bf16[8,18,1024]{2,1,0:T(8,128)(2,1)}), bf16[8,18,1024]{2,1,0:T(8,128)(2,1)S(1)}, u32[]{:S(2)}, u32[]{:S(2)}) async-start(bf16[8,18,1024]{2,1,0:T(8,128)(2,1)} %fusion.15), calls=%async_computation.1 | async-start | bytes 786432 | tf_op jit(solution)/shard_map/all_to_all | solution.py:152
  420.0 11.7 %all-to-all-done.1 = bf16[8,18,1024]{2,1,0:T(8,128)(2,1)S(1)} async-done(((bf16[8,18,1024]{2,1,0:T(8,128)(2,1)}), bf16[8,18,1024]{2,1,0:T(8,128)(2,1)S(1)}, u32[]{:S(2)}, u32[]{:S(2)}) %all-to-all-start.1) | async-done | bytes 294944 | tf_op jit(solution)/shard_map/all_to_all | solution.py:152
  431.8 0.8 gather_fusion
  432.9 0.8 multiply_reduce_fusion.1
  (72 shorter events, 10.5 us)
Async XLA Ops:
  6.5 413.1 %copy-start = (bf16[4096,8]{0,1:T(8,128)(2,1)S(1)}, bf16[4096,8]{0,1:T(8,128)(2,1)}, u32[]{:S(2)}) copy-start(bf16[4096,8]{0,1:T(8,128)(2,1)} %param.27) | copy-start | bytes 196612
  6.5 8.9 %copy-start.5 = (s32[1,64]{1,0:T(1,128)S(1)}, s32[1,64]{1,0:T(1,128)}, u32[]{:S(2)}) copy-start(s32[1,64]{1,0:T(1,128)} %param.25) | copy-start | bytes 772
  6.5 45.8 %copy-start.1 = (bf16[64,4096]{1,0:T(8,128)(2,1)S(1)}, bf16[64,4096]{1,0:T(8,128)(2,1)}, u32[]{:S(2)}) copy-start(bf16[64,4096]{1,0:T(8,128)(2,1)} %param.16) | copy-start | bytes 1572868
  6.5 45.8 %copy-start.2 = (f32[4096]{0:T(1024)S(1)}, f32[4096]{0:T(1024)}, u32[]{:S(2)}) copy-start(f32[4096]{0:T(1024)} %param.17) | copy-start | bytes 49156
  6.5 45.8 %all-gather.6.cloned.1.call-start = ((), (), s32[]{:S(2)}) async-start(), calls=%async_computation.2 | async-start | bytes 1179648 | tf_op jit(solution)/shard_map/all_gather | solution.py:115
  7.3 86.2 %all-gather.8.cloned.1.call-start = ((), (), s32[]{:S(2)}) async-start(), calls=%async_computation.3 | async-start | bytes 1179648 | tf_op jit(solution)/shard_map/all_gather | solution.py:114
  8.0 159.7 %all-gather.10.cloned.1.call-start = ((), (), s32[]{:S(2)}) async-start(), calls=%async_computation.4 | async-start | bytes 4718592 | tf_op jit(solution)/shard_map/all_gather | solution.py:113
  8.8 234.2 %all-gather.12.cloned.1.call-start = ((), (), s32[]{:S(2)}) async-start(), calls=%async_computation.5 | async-start | bytes 4718592 | tf_op jit(solution)/shard_map/all_gather | solution.py:116
  9.3 272.1 %all-reduce.2.cloned.1.call-start = ((), (), s32[]{:S(2)}) async-start(), calls=%async_computation.6 | async-start | bytes 2097152 | tf_op jit(solution)/shard_map/psum | solution.py:130
  95.2 76.0 %copy-start.6 = (bf16[8,256,128]{2,1,0:T(8,128)(2,1)S(1)}, bf16[8,256,128]{2,1,0:T(8,128)(2,1)}, u32[]{:S(2)}) copy-start(bf16[8,256,128]{2,1,0:T(8,128)(2,1)} %param.22) | copy-start | bytes 1572868
  171.2 1.1 copy-start.7
  247.0 35.9 %copy-start.3 = (f32[4096]{0:T(1024)S(1)}, f32[4096]{0:T(1024)}, u32[]{:S(2)}) copy-start(f32[4096]{0:T(1024)} %param.26) | copy-start | bytes 49156
  247.0 152.4 %all-gather.14.cloned.1.call-start = ((), (), s32[]{:S(2)}) async-start(), calls=%async_computation.7 | async-start | bytes 6881280 | tf_op jit(solution)/shard_map/all_gather | solution.py:147
  345.1 13.7 %copy-start.4 = (s32[64,2]{0,1:T(2,128)S(1)}, s32[64,2]{0,1:T(2,128)}, u32[]{:S(2)}) copy-start(s32[64,2]{0,1:T(2,128)} %param.28) | copy-start | bytes 1540
  414.1 17.6 %all-to-all-start.1 = ((bf16[8,18,1024]{2,1,0:T(8,128)(2,1)}), bf16[8,18,1024]{2,1,0:T(8,128)(2,1)S(1)}, u32[]{:S(2)}, u32[]{:S(2)}) async-start(bf16[8,18,1024]{2,1,0:T(8,128)(2,1)} %fusion.15), calls=%async_computation.1 | async-start | bytes 786432 | tf_op jit(solution)/shard_map/all_to_all | solution.py:152
Sparse Core Ops, SparseCore 0:
  9.5 42.8 all-gather.5
  54.5 38.8 all-gather.7
  95.6 72.1 all-gather.9
  169.7 73.2 all-gather.11
  247.1 34.2 all-reduce.1
  358.7 40.6 all-gather.13
where the time goes:
time: 442 us; the launch traced here: 441 us
  waiting for transfers between devices  308 us (70%)
  matrix products  52.4 us (12%)
  blocking collectives  41.9 us (9%)
  between operations  13.8 us (3%)
  local copies, waits for them, and re-layouts  10.5 us (2%)
  other arithmetic  9.38 us (2%)
  starting transfers between devices  5.74 us (1%)
    all_gather x1, waiting for transfers between devices, shards(): lax.all_gather(q_weight, 'tok', axis=0, tiled=True)  72.5 us
    all_gather x1, waiting for transfers between devices, shards(): lax.all_gather(output_matrix, 'tok', axis=1, tiled=True)  70 us
    all_to_all x1, blocking collectives, shards(): lax.all_to_all(outgoing, 'tok', split_axis=0, concat_axis=0, tiled=True)  41.9 us
    all_gather x1, waiting for transfers between devices, shards(): hidden_all = lax.all_gather(hidden, 'head', axis=2, tiled=True)  40.4 us
    all_gather x1, waiting for transfers between devices, shards(): lax.all_gather(k_weight, 'tok', axis=0, tiled=True)  39.5 us
    all_gather x1, waiting for transfers between devices, shards(): lax.all_gather(v_weight, 'tok', axis=0, tiled=True)  36.7 us
    psum x1, waiting for transfers between devices, shards(): mixed = lax.psum(partial_mix, 'head')  34.1 us
    dot_general x1, matrix products, shards(): jnp.einsum('tcf,fd->tcd', hidden_all, down_weight[0], preferred_element_t...  14.7 us
  transfers between devices with their start and end apart: 7, of which 7 were waited for; matrix products, arithmetic and copies ran while one was open for 4% of the time, Pallas kernels for 0%

commit v1 on v0

--- a/solution.py
+++ b/solution.py
@@ -144,7 +144,12 @@
     active = jnp.einsum("tcd,df->tcf", arrived, gate_weight[0], preferred_element_type=jnp.float32)
     linear = jnp.einsum("tcd,df->tcf", arrived, up_weight[0], preferred_element_type=jnp.float32)
     hidden = (jax.nn.silu(active) * linear).astype(jnp.bfloat16)
-    hidden_all = lax.all_gather(hidden, "head", axis=2, tiled=True)
+    ring = [hidden]
+    for hop in range(3):
+        ring.append(lax.ppermute(ring[-1], "head", [(dev, (dev + 1) % 4) for dev in range(4)]))
+    hidden_all = jnp.roll(
+        jnp.concatenate(ring[::-1], axis=2), (lax.axis_index("head") + 1) * ring[0].shape[2], axis=2
+    )
     output = jnp.einsum(
         "tcf,fd->tcd", hidden_all, down_weight[0], preferred_element_type=jnp.float32
     )

time: 442 us -> 457 us (1.034)
  local copies, waits for them, and re-layouts: 10.5 us -> 27.8 us
    ppermute x0 -> x3, waiting for transfers between devices: none -> 42.2 us  [shards(): lax.ppermute(ring[-1], 'head', [(dev, (dev + 1) % 4) for dev in range(4)])]
    all_gather x1 -> x0, waiting for transfers between devices: 40.4 us -> none  [shards(): hidden_all = lax.all_gather(hidden, 'head', axis=2, tiled=True)]
    unnamed x17 -> x26, local copies, waits for them, and re-layouts: 0.81 us -> 16.6 us
  transfers between devices with their start and end apart: 7 -> 9, of which waited for: 7 -> 9; matrix products, arithmetic and copies ran while one was open for 4% -> 4% of each run, Pallas kernels for 0% -> 0%
where the time goes in v1:
time: 457 us; the launch traced here: 456 us
  waiting for transfers between devices  307 us (67%)
  matrix products  51.7 us (11%)
  blocking collectives  41.9 us (9%)
  local copies, waits for them, and re-layouts  27.8 us (6%)
  between operations  13.5 us (3%)
  other arithmetic  10 us (2%)
    all_gather x1, waiting for transfers between devices, shards(): lax.all_gather(q_weight, 'tok', axis=0, tiled=True)  72.5 us
    all_gather x1, waiting for transfers between devices, shards(): lax.all_gather(output_matrix, 'tok', axis=1, tiled=True)  70 us
    ppermute x3, waiting for transfers between devices, shards(): lax.ppermute(ring[-1], 'head', [(dev, (dev + 1) % 4) for dev in range(4)])  42.2 us
    all_to_all x1, blocking collectives, shards(): lax.all_to_all(outgoing, 'tok', split_axis=0, concat_axis=0, tiled=True)  41.9 us
    all_gather x1, waiting for transfers between devices, shards(): lax.all_gather(k_weight, 'tok', axis=0, tiled=True)  39.3 us
    all_gather x1, waiting for transfers between devices, shards(): lax.all_gather(v_weight, 'tok', axis=0, tiled=True)  36.1 us
    psum x1, waiting for transfers between devices, shards(): mixed = lax.psum(partial_mix, 'head')  34.2 us
    unnamed x26, local copies, waits for them, and re-layouts  16.6 us
  transfers between devices with their start and end apart: 9, of which 9 were waited for; matrix products, arithmetic and copies ran while one was open for 4% of the time, Pallas kernels for 0%

profile of v1, /device:TPU:0, one launch (start us, length us, event | category | flops | bytes accessed | tf_op | source)
XLA Modules:
  0.0 456.0 jit_solution(1126135301547903132)
XLA Ops:
  16.3 36.1 %all-gather.5.cloned.1.call-done = bf16[4096,128]{1,0:T(8,128)(2,1)} async-done(((bf16[512,128]{1,0:T(8,128)(2,1)}), bf16[4096,128]{1,0:T(8,128)(2,1)}) %all-gather.5.cloned.1.call-update) | async-done | bytes 1048592 | tf_op jit(solution)/shard_map/all_gather | solution.py:115
  52.4 1.7 fusion.23
  54.1 39.3 %all-gather.7.cloned.1.call-done = bf16[4096,128]{1,0:T(8,128)(2,1)} async-done(((bf16[512,128]{1,0:T(8,128)(2,1)}), bf16[4096,128]{1,0:T(8,128)(2,1)}) %all-gather.7.cloned.1.call-update) | async-done | bytes 1048592 | tf_op jit(solution)/shard_map/all_gather | solution.py:114
  93.4 1.6 fusion.61
  95.2 72.5 %all-gather.9.cloned.1.call-done = bf16[4096,512]{1,0:T(8,128)(2,1)} async-done(((bf16[512,512]{1,0:T(8,128)(2,1)}), bf16[4096,512]{1,0:T(8,128)(2,1)}) %all-gather.9.cloned.1.call-update) | async-done | bytes 4194320 | tf_op jit(solution)/shard_map/all_gather | solution.py:113
  167.8 3.1 fusion.59
  172.9 70.0 %all-gather.11.cloned.1.call-done = bf16[512,4096]{1,0:T(8,128)(2,1)} async-done(((bf16[512,512]{1,0:T(8,128)(2,1)}), bf16[512,4096]{1,0:T(8,128)(2,1)}) %all-gather.11.cloned.1.call-update) | async-done | bytes 4194320 | tf_op jit(solution)/shard_map/all_gather | solution.py:116
  243.0 4.0 fusion.36
  247.2 34.2 %all-reduce.2.cloned.1.call-done = f32[64,4096]{1,0:T(8,128)} async-done(((f32[64,4096]{1,0:T(8,128)}), f32[64,4096]{1,0:T(8,128)}) %all-reduce.2.cloned.1.call-update) | async-done | bytes 1048592 | tf_op jit(solution)/shard_map/psum | solution.py:130
  283.0 6.1 %scatter_custom_fusion = bf16[144,4096]{1,0:T(8,128)(2,1)} fusion(s32[128]{0:T(128)S(1)} %fusion.55, bf16[64,4096]{1,0:T(8,128)(2,1)S(1)} %multiply_convert_fusion, s32[1024]{0:T(1024)S(1)} %pad_clamp_fusion.1, bf16[]{:T(256)} %constant.122.clone.1), kind=kCustom, calls=%fused_computation.36 | custom fusion | bytes 1179650 | tf_op jit(solution)/shard_map/scatter | solution.py:81
  290.7 41.9 %all_to_all.10 = bf16[8,18,4096]{2,1,0:T(8,128)(2,1)S(1)} all-to-all(bf16[8,18,4096]{2,1,0:T(8,128)(2,1)S(1)} %reshape_reshape.3), channel_id=1, replica_groups=mesh['head'=4,'tok'=8] {'tok'}, dimensions={0} | all-to-all | bytes 2359296 | tf_op jit(solution)/shard_map/all_to_all | solution.py:143
  332.5 12.5 %fusion.4 = f32[8,18,3584]{2,1,0:T(8,128)S(1)} fusion(bf16[8,18,4096]{2,1,0:T(8,128)(2,1)S(1)} %all_to_all.10, bf16[1,4096,3584]{2,1,0:T(8,128)(2,1)} %param.29), kind=kOutput, calls=%fused_computation.7 | convolution fusion | flops 4227858432 | bytes 32604160 | tf_op jit(solution)/shard_map/tcd,df->tcf/dot_general | solution.py:144
  345.1 12.6 %fusion.10 = bf16[8,18,3584]{2,1,0:T(8,128)(2,1)S(1)} fusion(bf16[8,18,4096]{2,1,0:T(8,128)(2,1)S(1)} %all_to_all.10, bf16[1,4096,3584]{2,1,0:T(8,128)(2,1)} %param.30, f32[8,18,3584]{2,1,0:T(8,128)S(1)} %fusion.4), kind=kOutput, calls=%fused_computation.11 | convolution fusion | flops 4230955008 | bytes 33636352 | tf_op jit(solution)/shard_map/tcd,df->tcf/dot_general | solution.py:145
  358.1 14.0 %collective-permute-done = bf16[8,18,3584]{2,0,1:T(8,128)(2,1)S(1)} collective-permute-done((bf16[8,18,3584]{2,0,1:T(8,128)(2,1)S(1)}, bf16[8,18,3584]{2,0,1:T(8,128)(2,1)S(1)}, u32[]{:S(2)}, u32[]{:S(2)}) %collective-permute-start) | collective-permute-done | bytes 1032224 | tf_op jit(solution)/shard_map/ppermute | solution.py:149
  373.1 14.2 %collective-permute-done.1 = bf16[8,18,3584]{2,0,1:T(8,128)(2,1)} collective-permute-done((bf16[8,18,3584]{2,0,1:T(8,128)(2,1)S(1)}, bf16[8,18,3584]{2,0,1:T(8,128)(2,1)}, u32[]{:S(2)}, u32[]{:S(2)}) %collective-permute-start.1) | collective-permute-done | bytes 1032224 | tf_op jit(solution)/shard_map/ppermute | solution.py:149
  387.7 14.0 %collective-permute-done.2 = bf16[8,18,3584]{2,0,1:T(8,128)(2,1)} collective-permute-done((bf16[8,18,3584]{2,0,1:T(8,128)(2,1)}, bf16[8,18,3584]{2,0,1:T(8,128)(2,1)}, u32[]{:S(2)}, u32[]{:S(2)}) %collective-permute-start.2) | collective-permute-done | bytes 1032224 | tf_op jit(solution)/shard_map/ppermute | solution.py:149
  401.7 2.6 copy_dynamic-update-slice_fusion.4
  404.3 2.7 copy_dynamic-update-slice_fusion.2
  409.7 2.6 copy_dynamic-update-slice_fusion.5
  412.3 2.7 copy_dynamic-update-slice_fusion.3
  415.0 1.5 copy_dynamic-update-slice_fusion.1
  417.7 14.8 %fusion.16 = bf16[8,18,1024]{2,1,0:T(8,128)(2,1)} fusion(bf16[1,14336,1024]{2,1,0:T(8,128)(2,1)} %param.31, bf16[8,18,28672]{2,1,0:T(8,128)(2,1)} %constant_dynamic-update-slice_fusion, s32[]{:T(128)S(6)} %select_n.103), kind=kOutput, calls=%fused_computation.27 | convolution fusion | flops 4228005888 | bytes 35160068 | tf_op jit(solution)/shard_map/tcf,fd->tcd/dot_general | solution.py:153
  432.4 3.5 all-to-all-start.1
  436.4 10.4 %all-to-all-done.1 = bf16[8,18,1024]{2,1,0:T(8,128)(2,1)S(1)} async-done(((bf16[8,18,1024]{2,1,0:T(8,128)(2,1)}), bf16[8,18,1024]{2,1,0:T(8,128)(2,1)S(1)}, u32[]{:S(2)}, u32[]{:S(2)}) %all-to-all-start.1) | async-done | bytes 294944 | tf_op jit(solution)/shard_map/all_to_all | solution.py:157
  (86 shorter events, 23.9 us)
Async XLA Ops:
  6.5 429.5 %copy-start = (bf16[4096,8]{0,1:T(8,128)(2,1)S(1)}, bf16[4096,8]{0,1:T(8,128)(2,1)}, u32[]{:S(2)}) copy-start(bf16[4096,8]{0,1:T(8,128)(2,1)} %param.27) | copy-start | bytes 196612
  6.5 86.9 %copy-start.1 = (bf16[64,4096]{1,0:T(8,128)(2,1)S(1)}, bf16[64,4096]{1,0:T(8,128)(2,1)}, u32[]{:S(2)}) copy-start(bf16[64,4096]{1,0:T(8,128)(2,1)} %param.16) | copy-start | bytes 1572868
  6.5 86.9 %copy-start.4 = (f32[4096]{0:T(1024)S(1)}, f32[4096]{0:T(1024)}, u32[]{:S(2)}) copy-start(f32[4096]{0:T(1024)} %param.17) | copy-start | bytes 49156
  6.5 45.8 %all-gather.5.cloned.1.call-start = ((), (), s32[]{:S(2)}) async-start(), calls=%async_computation.2 | async-start | bytes 1179648 | tf_op jit(solution)/shard_map/all_gather | solution.py:115
  7.3 86.2 %all-gather.7.cloned.1.call-start = ((), (), s32[]{:S(2)}) async-start(), calls=%async_computation.3 | async-start | bytes 1179648 | tf_op jit(solution)/shard_map/all_gather | solution.py:114
  8.0 159.7 %all-gather.9.cloned.1.call-start = ((), (), s32[]{:S(2)}) async-start(), calls=%async_computation.4 | async-start | bytes 4718592 | tf_op jit(solution)/shard_map/all_gather | solution.py:113
  8.7 234.2 %all-gather.11.cloned.1.call-start = ((), (), s32[]{:S(2)}) async-start(), calls=%async_computation.5 | async-start | bytes 4718592 | tf_op jit(solution)/shard_map/all_gather | solution.py:116
  9.3 272.1 %all-reduce.2.cloned.1.call-start = ((), (), s32[]{:S(2)}) async-start(), calls=%async_computation.6 | async-start | bytes 2097152 | tf_op jit(solution)/shard_map/psum | solution.py:130
  95.2 76.0 %copy-start.7 = (bf16[8,256,128]{2,1,0:T(8,128)(2,1)S(1)}, bf16[8,256,128]{2,1,0:T(8,128)(2,1)}, u32[]{:S(2)}) copy-start(bf16[8,256,128]{2,1,0:T(8,128)(2,1)} %param.22) | copy-start | bytes 1572868
  171.2 1.1 copy-start.8
  247.0 35.9 %copy-start.5 = (f32[4096]{0:T(1024)S(1)}, f32[4096]{0:T(1024)}, u32[]{:S(2)}) copy-start(f32[4096]{0:T(1024)} %param.26) | copy-start | bytes 49156
  345.1 42.5 %copy-start.6 = (s32[64,2]{0,1:T(2,128)S(1)}, s32[64,2]{0,1:T(2,128)}, u32[]{:S(2)}) copy-start(s32[64,2]{0,1:T(2,128)} %param.28) | copy-start | bytes 1540
  358.0 14.1 %collective-permute-start = (bf16[8,18,3584]{2,0,1:T(8,128)(2,1)S(1)}, bf16[8,18,3584]{2,0,1:T(8,128)(2,1)S(1)}, u32[]{:S(2)}, u32[]{:S(2)}) collective-permute-start(bf16[8,18,3584]{2,0,1:T(8,128)(2,1)S(1)} %copy.60), channel_id=1, source_target_pairs={{0,8},{8,16},{16,24},{24,0},{1,9},{9,17},{17,25},{25,1},{2,10},{10... | collective-permute-start | bytes 3096584 | tf_op jit(solution)/shard_map/ppermute | solution.py:149
  372.1 1.0 copy-start.2
  373.1 14.2 %collective-permute-start.1 = (bf16[8,18,3584]{2,0,1:T(8,128)(2,1)S(1)}, bf16[8,18,3584]{2,0,1:T(8,128)(2,1)}, u32[]{:S(2)}, u32[]{:S(2)}) collective-permute-start(bf16[8,18,3584]{2,0,1:T(8,128)(2,1)S(1)} %collective-permute-done), channel_id=1, source_target_pairs={{0,8},{8,16},{16,24},{24,0},{1,9},{9,17},{17,25},{25,1},{2,10},{10... | collective-permute-start | bytes 3096584 | tf_op jit(solution)/shard_map/ppermute | solution.py:149
  387.3 14.4 %collective-permute-start.2 = (bf16[8,18,3584]{2,0,1:T(8,128)(2,1)}, bf16[8,18,3584]{2,0,1:T(8,128)(2,1)}, u32[]{:S(2)}, u32[]{:S(2)}) collective-permute-start(bf16[8,18,3584]{2,0,1:T(8,128)(2,1)} %collective-permute-done.1), channel_id=1, source_target_pairs={{0,8},{8,16},{16,24},{24,0},{1,9},{9,17},{17,25},{25,1},{2,10},{10... | collective-permute-start | bytes 3096584 | tf_op jit(solution)/shard_map/ppermute | solution.py:149
  387.7 19.3 %copy-start.3 = (bf16[8,18,3584]{2,0,1:T(8,128)(2,1)S(1)}, bf16[8,18,3584]{2,0,1:T(8,128)(2,1)}, u32[]{:S(2)}) copy-start(bf16[8,18,3584]{2,0,1:T(8,128)(2,1)} %copy-done.2) | copy-start | bytes 3096580
  432.4 14.3 %all-to-all-start.1 = ((bf16[8,18,1024]{2,1,0:T(8,128)(2,1)}), bf16[8,18,1024]{2,1,0:T(8,128)(2,1)S(1)}, u32[]{:S(2)}, u32[]{:S(2)}) async-start(bf16[8,18,1024]{2,1,0:T(8,128)(2,1)} %fusion.16), calls=%async_computation.1 | async-start | bytes 786432 | tf_op jit(solution)/shard_map/all_to_all | solution.py:157
Sparse Core Ops, SparseCore 0:
  9.5 42.8 all-gather.4
  54.5 38.8 all-gather.6
  95.6 72.1 all-gather.8
  169.6 73.2 all-gather.10
  247.1 34.2 all-reduce.1
